TPU v7x, 256 devices: a whole 4x4x8 slice. The times are simulated.
256 devices in a mesh: enc: 4 (over z_lo), lab: 64 (over z_hi, y, x, core).
Axes of the slice: x: 4, y: 4, z: 8 (z_hi: 2, z_lo: 4; z = z_hi * 4 + z_lo), core: 2. Of those that a mesh axis runs over, the one named last changes fastest.
Arguments:
- embeddings: bfloat16 [131072, 768], P(('enc', 'lab')), may hold values from -6 to 6
- classifier: float32 [4096, 768], P('lab'), may hold values from -0.21875 to 0.21875
- label_valid: int32 [4096], P('lab'), may hold values 0 or 1
- shortlist: int32 [131072, 4], P(('enc', 'lab')), may hold values from 0 to 63, all different within a row; in each aligned block of 512 rows (0 to 511, 512 to 1023, ...) at most 48 rows name the same one
- slot_live: int32 [131072, 4], P(('enc', 'lab')), may hold values 0 or 1
- positive: int32 [131072, 4], P(('enc', 'lab')), may hold values from 0 to 63
- negative: int32 [131072, 4, 8], P(('enc', 'lab')), may hold values from 0 to 63
Outputs:
- w_grad: float32 [4096, 768], P('lab')
- emb_grad: float32 [131072, 768], P(('enc', 'lab'))
Inputs may be any that keep to these rules, and one draw needn't show every extreme that they name: `shortlist`: each document names 4 different clusters; among the 512 documents of one device no cluster is named by more than 48 documents.
All inputs are finite; a program needn't handle non-finite values. No bound on the sum of `label_valid` or of `slot_live` on one device may be relied on, other than what follows from the above.
Results may differ from a plain program's by a relative error of at most 0.0041.
Values may be sent and summed in bfloat16 or wider, within the bound.
A program may use at most 128 MiB of HBM per device.

v0:
```python
import math
import jax
import jax.numpy as jnp
from jax import lax
from jax.sharding import PartitionSpec as P


def dense_targets(shortlist, slot_live, positive, negative, clusters, panel):
    labels = jnp.arange(panel, dtype=jnp.int32)
    pos_hot = (positive[..., None] == labels).astype(jnp.float32)
    neg_count = jnp.sum((negative[..., None] == labels).astype(jnp.float32), axis=2)
    live = slot_live.astype(jnp.float32)[..., None]
    slot_weight = live * (pos_hot + neg_count)
    cluster_hot = (shortlist[..., None] == jnp.arange(clusters, dtype=jnp.int32)).astype(
        jnp.float32
    )
    count = shortlist.shape[0]
    weight = jnp.einsum("nsc,nsj->ncj", cluster_hot, slot_weight).reshape(count, clusters * panel)
    target = jnp.einsum("nsc,nsj->ncj", cluster_hot, pos_hot).reshape(count, clusters * panel)
    return (weight.astype(jnp.bfloat16), target.astype(jnp.bfloat16))


def make_absorb(embeddings, weight_all, target_all):

    def absorb(carry, pieces, start):
        w_piece, v_piece = pieces
        weight = weight_all.astype(jnp.float32)
        weight = weight * v_piece.astype(jnp.float32)[None, :]
        target = target_all.astype(jnp.float32)
        logits = lax.dot_general(
            embeddings, w_piece, (((1,), (1,)), ((), ())), preferred_element_type=jnp.float32
        )
        dlogits = (weight * (jax.nn.sigmoid(logits) - target)).astype(jnp.bfloat16)
        grad_acc = jnp.dot(dlogits, w_piece, preferred_element_type=jnp.float32)
        return (grad_acc, dlogits)

    return absorb


def shards(embeddings, classifier, label_valid, shortlist, slot_live, positive, negative):
    lab_count = lax.axis_size("lab")
    enc_count = lax.axis_size("enc")
    docs, width = embeddings.shape
    panel = classifier.shape[0]
    slots = shortlist.shape[1]
    classifier_b = classifier.astype(jnp.bfloat16)
    weight_all, target_all = dense_targets(
        shortlist, slot_live, positive, negative, lab_count, panel
    )
    absorb = make_absorb(embeddings, weight_all, target_all)
    initial = (
        jnp.zeros((docs, width), jnp.float32),
        jnp.zeros((docs, lab_count * panel), jnp.bfloat16),
    )
    emb_grad, scored = absorb(
        initial,
        (
            lax.all_gather(classifier_b, "lab", axis=0, tiled=True),
            lax.all_gather(label_valid.astype(jnp.bfloat16), "lab", axis=0, tiled=True),
        ),
        jnp.int32(0),
    )
    partial_grad = lax.psum_scatter(
        lax.dot_general(
            scored, embeddings, (((0,), (0,)), ((), ())), preferred_element_type=jnp.float32
        ),
        "lab",
        scatter_dimension=0,
        tiled=True,
    )
    scale_factor = 1.0 / math.sqrt(docs * enc_count * slots)
    w_grad = lax.psum(partial_grad, "enc") * scale_factor
    return (w_grad, emb_grad)


def solution(mesh):
    in_specs = (
        P(("enc", "lab"), None),
        P("lab", None),
        P("lab"),
        P(("enc", "lab"), None),
        P(("enc", "lab"), None),
        P(("enc", "lab"), None),
        P(("enc", "lab"), None, None),
    )
    out_specs = (P("lab", None), P(("enc", "lab"), None))
    return jax.shard_map(shards, mesh=mesh, in_specs=in_specs, out_specs=out_specs, check_vma=False)
```

profile of v0, /device:TPU:2, one launch (start us, length us, event | category | flops | bytes accessed | tf_op | source)
XLA Modules:
  0.0 586.9 jit_solution(4797817930439539385)
XLA Ops:
  7.2 0.0 copy-start
  7.2 0.0 all-gather.2.cloned.1.call-start
  7.2 1.6 convert_element_type.50
  8.9 0.0 all-gather.2.cloned.1.call-update
  8.9 0.0 reduce-scatter.2.cloned.1.call-start
  8.9 0.8 copy.21
  9.8 0.7 convert_element_type.42
  10.5 1.4 convert_reduce_fusion
  11.9 0.8 add_multiply_fusion
  12.7 0.3 copy.22
  13.0 8.6 %convert_convert_fusion.1 = f32[512,64,64]{2,1,0:T(8,128)} fusion(bf16[512,4,64]{2,1,0:T(4,128)(2,1)S(1)} %copy.22, s32[512,4]{1,0:T(8,128)S(1)} %copy.21), kind=kOutput, calls=%fused_computation.2 | convolution fusion | flops 19005440 | bytes 8658944 | tf_op jit(solution)/shard_map/nsc,nsj->ncj/dot_general | solution.py:18
  21.6 12.8 %copy.23 = f32[512,64,64]{0,2,1:T(8,128)} copy(f32[512,64,64]{2,1,0:T(8,128)} %convert_convert_fusion.1) | data formatting | bytes 16777216 | tf_op jit(solution)/shard_map/convert_element_type | solution.py:27
  34.4 0.0 copy-start.1
  34.4 8.9 %copy.24 = f32[512,4096]{1,0:T(8,128)} copy(f32[512,4096]{0,1:T(8,128)} %bitcast.11) | data formatting | bytes 16777216 | tf_op jit(solution)/shard_map/convert_element_type | solution.py:27
  43.3 0.0 copy-done.1
  43.4 0.1 iota_compare_fusion.4
  43.4 0.4 copy.25
  43.9 8.7 %convert_convert_fusion = f32[512,64,64]{2,1,0:T(8,128)} fusion(pred[512,4,64]{2,1,0:T(4,128)(4,1)S(1)} %copy.25, s32[512,4]{1,0:T(8,128)S(1)} %copy.21), kind=kOutput, calls=%fused_computation.1 | convolution fusion | flops 21102592 | bytes 8527872 | tf_op jit(solution)/shard_map/nsc,nsj->ncj/dot_general | solution.py:19
  52.5 12.8 %copy.26 = f32[512,64,64]{0,2,1:T(8,128)} copy(f32[512,64,64]{2,1,0:T(8,128)} %convert_convert_fusion) | data formatting | bytes 16777216 | tf_op jit(solution)/shard_map/convert_element_type | solution.py:29
  65.3 0.0 copy-start.2
  65.3 0.0 copy-start.3
  65.3 9.0 %copy.27 = f32[512,4096]{1,0:T(8,128)} copy(f32[512,4096]{0,1:T(8,128)} %bitcast.12) | data formatting | bytes 16777216 | tf_op jit(solution)/shard_map/convert_element_type | solution.py:29
  74.3 0.0 copy-done.2
  74.3 0.0 copy-done.3
  74.3 0.6 dynamic-slice
  75.5 0.2 dynamic-update-slice
  75.8 205.7 %all-reduce = bf16[4096]{0:T(1024)(128)(2,1)S(1)} all-reduce(bf16[4096]{0:T(1024)(128)(2,1)S(1)} %dynamic-update-slice), channel_id=1, replica_groups=mesh['enc'=4,'lab'=64] {'lab'}, use_global_device_ids=true, to_apply=%add | all-reduce | flops 4096 | bytes 16384
  281.5 0.0 all-gather.2.cloned.1.call-done
  281.5 0.0 copy-done
  281.6 11.0 %multiply_convert_fusion = bf16[512,4096]{1,0:T(8,128)(2,1)} fusion(f32[512,4096]{1,0:T(8,128)} %copy.27, f32[512,4096]{1,0:T(8,128)} %copy.24, bf16[512,768]{1,0:T(8,128)(2,1)S(1)} %copy-done, bf16[4096,768]{1,0:T(8,128)(2,1)} %all-gather.2.cloned.1.call-done, f32[4096]{0:T(1024)S(1)} %convert_element_type.49), kind=kOutput, calls=%fused_computation | convolution fusion | flops 3235905536 | bytes 28065792 | tf_op jit(solution)/shard_map/dot_general | solution.py:30
  292.5 10.2 %fusion.2 = f32[4096,768]{1,0:T(8,128)} fusion(bf16[512,4096]{1,0:T(8,128)(2,1)} %multiply_convert_fusion, bf16[512,768]{1,0:T(8,128)(2,1)S(1)} %copy-done), kind=kOutput, calls=%fused_computation.11 | convolution fusion | flops 3221225472 | bytes 17563648 | tf_op jit(solution)/shard_map/dot_general | solution.py:64
  302.8 0.0 reduce-scatter.2.cloned.1.call-update
  302.8 0.0 all-reduce.3.cloned.1.call-start
  302.8 228.7 %reduce-scatter.2.cloned.1.call-done = f32[64,768]{1,0:T(8,128)} async-done(((f32[4096,768]{1,0:T(8,128)}), f32[64,768]{1,0:T(8,128)}) %reduce-scatter.2.cloned.1.call-update) | async-done | bytes 196624 | tf_op jit(solution)/shard_map/reduce_scatter | solution.py:63
  531.6 0.0 all-reduce.3.cloned.1.call-update
  531.6 8.6 %fusion.3 = f32[512,768]{1,0:T(8,128)} fusion(bf16[512,4096]{1,0:T(8,128)(2,1)} %multiply_convert_fusion, bf16[4096,768]{1,0:T(8,128)(2,1)} %all-gather.2.cloned.1.call-done), kind=kOutput, calls=%fused_computation.12 | convolution fusion | flops 3221225472 | bytes 12058624 | tf_op jit(solution)/shard_map/dot_general | solution.py:34
  540.2 38.6 %all-reduce.3.cloned.1.call-done = f32[64,768]{1,0:T(8,128)} async-done(((f32[64,768]{1,0:T(8,128)}), f32[64,768]{1,0:T(8,128)}) %all-reduce.3.cloned.1.call-update) | async-done | bytes 196624 | tf_op jit(solution)/shard_map/psum | solution.py:72
  578.8 1.6 broadcast_multiply_fusion
  (3 shorter events, 0.0 us)
Async XLA Ops:
  7.2 274.4 %copy-start = (bf16[512,768]{1,0:T(8,128)(2,1)S(1)}, bf16[512,768]{1,0:T(8,128)(2,1)}, u32[]{:S(2)}) copy-start(bf16[512,768]{1,0:T(8,128)(2,1)} %param.7) | copy-start | bytes 2359300
  7.2 274.4 %all-gather.2.cloned.1.call-start = ((), (), s32[]{:S(2)}) async-start(), calls=%async_computation.1 | async-start | bytes 6389760 | tf_op jit(solution)/shard_map/all_gather | solution.py:58
  8.9 522.7 %reduce-scatter.2.cloned.1.call-start = ((), (), s32[]{:S(2)}) async-start(), calls=%async_computation.2 | async-start | bytes 12779520 | tf_op jit(solution)/shard_map/reduce_scatter | solution.py:63
  34.4 9.0 %copy-start.1 = (s32[512,4]{0,1:T(4,128)S(1)}, s32[512,4]{0,1:T(4,128)}, u32[]{:S(2)}) copy-start(s32[512,4]{0,1:T(4,128)} %param.12) | copy-start | bytes 24580
  65.3 9.0 %copy-start.2 = (s32[64]{0:T(128)S(1)}, s32[64]{0:T(128)}, u32[]{:S(2)}) copy-start(s32[64]{0:T(128)} %param.9) | copy-start | bytes 772
  65.3 9.0 %copy-start.3 = (u32[256]{0:T(256)S(1)}, u32[256]{0:T(256)}, u32[]{:S(2)}) copy-start(u32[256]{0:T(256)} %constant.8) | copy-start | bytes 3076
  302.8 276.0 %all-reduce.3.cloned.1.call-start = ((), (), s32[]{:S(2)}) async-start(), calls=%async_computation.3 | async-start | bytes 393216 | tf_op jit(solution)/shard_map/psum | solution.py:72
Sparse Core Ops, SparseCore 0:
  12.3 104.1 all-gather.1
  302.9 228.6 reduce-scatter.1
  534.2 44.5 all-reduce.2
where the time goes:
time: 588 us; the launch traced here: 587 us
  waiting for transfers between devices  267 us (45%)
  blocking collectives  206 us (35%)
  matrix products  47 us (8%)
  local copies, waits for them, and re-layouts  45.9 us (8%)
  between operations  14.5 us (2%)
  other arithmetic  6.25 us (1%)
    reduce_scatter x1, waiting for transfers between devices, shards(): lax.psum_scatter(lax.dot_general(scored, embeddings, (((0,), (0,)), ((),...  229 us
    unnamed x1, blocking collectives  206 us
    psum x1, waiting for transfers between devices, shards(): w_grad = lax.psum(partial_grad, 'enc') * scale_factor  38.6 us
    convert_element_type x2, local copies, waits for them, and re-layouts, absorb(): weight = weight_all.astype(jnp.float32)  21.8 us
    convert_element_type x2, local copies, waits for them, and re-layouts, absorb(): target = target_all.astype(jnp.float32)  21.7 us
  transfers between devices with their start and end apart: 3, of which 2 were waited for; matrix products, arithmetic and copies ran while one was open for 13% of the time, Pallas kernels for 0%

commit v1 on v0

--- a/solution.py
+++ b/solution.py
@@ -69,7 +69,7 @@
         tiled=True,
     )
     scale_factor = 1.0 / math.sqrt(docs * enc_count * slots)
-    w_grad = lax.psum(partial_grad, "enc") * scale_factor
+    w_grad = jnp.sum(lax.all_gather(partial_grad, "enc"), axis=0) * scale_factor
     return (w_grad, emb_grad)
 
 

time: 588 us -> 558 us (0.949)
  waiting for transfers between devices: 267 us -> 220 us
  blocking collectives: 206 us -> 224 us
    psum x1 -> x0, waiting for transfers between devices: 38.6 us -> none  [shards(): w_grad = lax.psum(partial_grad, 'enc') * scale_factor]
    all_gather x0 -> x1, blocking collectives: none -> 17.8 us  [shards(): w_grad = jnp.sum(lax.all_gather(partial_grad, 'enc'), axis=0) * scale_factor]
    reduce_scatter x1, waiting for transfers between devices: 229 us -> 220 us  [shards(): lax.psum_scatter(lax.dot_general(scored, embeddings, (((0,), (0,)), ((),...]
  transfers between devices with their start and end apart: 3 -> 2, of which waited for: 2 -> 1; matrix products, arithmetic and copies ran while one was open for 13% -> 13% of each run, Pallas kernels for 0% -> 0%
where the time goes in v1:
time: 558 us; the launch traced here: 557 us
  blocking collectives  224 us (40%)
  waiting for transfers between devices  220 us (39%)
  matrix products  47.1 us (8%)
  local copies, waits for them, and re-layouts  45.9 us (8%)
  between operations  14.8 us (3%)
    reduce_scatter x1, waiting for transfers between devices, shards(): lax.psum_scatter(lax.dot_general(scored, embeddings, (((0,), (0,)), ((),...  220 us
    unnamed x1, blocking collectives  206 us
    convert_element_type x2, local copies, waits for them, and re-layouts, absorb(): target = target_all.astype(jnp.float32)  21.7 us
    convert_element_type x2, local copies, waits for them, and re-layouts, absorb(): weight = weight_all.astype(jnp.float32)  21.7 us
    all_gather x1, blocking collectives, shards(): w_grad = jnp.sum(lax.all_gather(partial_grad, 'enc'), axis=0) * scale_factor  17.8 us
  transfers between devices with their start and end apart: 2, of which 1 were waited for; matrix products, arithmetic and copies ran while one was open for 13% of the time, Pallas kernels for 0%

profile of v1, /device:TPU:2, one launch (start us, length us, event | category | flops | bytes accessed | tf_op | source)
XLA Modules:
  0.0 557.0 jit_solution(889268817074462111)
XLA Ops:
  7.2 0.0 copy-start
  7.2 0.0 all-gather.3.cloned.1.call-start
  7.2 1.6 convert_element_type.50
  8.9 0.0 all-gather.3.cloned.1.call-update
  8.9 0.0 reduce-scatter.2.cloned.1.call-start
  8.9 0.8 copy.21
  9.8 0.7 convert_element_type.42
  10.5 1.4 convert_reduce_fusion
  11.9 0.8 add_multiply_fusion
  12.7 0.3 copy.22
  13.0 8.6 %convert_convert_fusion.1 = f32[512,64,64]{2,1,0:T(8,128)} fusion(bf16[512,4,64]{2,1,0:T(4,128)(2,1)S(1)} %copy.22, s32[512,4]{1,0:T(8,128)S(1)} %copy.21), kind=kOutput, calls=%fused_computation.2 | convolution fusion | flops 19005440 | bytes 8658944 | tf_op jit(solution)/shard_map/nsc,nsj->ncj/dot_general | solution.py:18
  21.6 12.8 %copy.23 = f32[512,64,64]{0,2,1:T(8,128)} copy(f32[512,64,64]{2,1,0:T(8,128)} %convert_convert_fusion.1) | data formatting | bytes 16777216 | tf_op jit(solution)/shard_map/convert_element_type | solution.py:27
  34.4 0.0 copy-start.1
  34.4 8.9 %copy.24 = f32[512,4096]{1,0:T(8,128)} copy(f32[512,4096]{0,1:T(8,128)} %bitcast.12) | data formatting | bytes 16777216 | tf_op jit(solution)/shard_map/convert_element_type | solution.py:27
  43.3 0.0 copy-done.1
  43.3 0.1 iota_compare_fusion.4
  43.4 0.4 copy.25
  43.9 8.7 %convert_convert_fusion = f32[512,64,64]{2,1,0:T(8,128)} fusion(pred[512,4,64]{2,1,0:T(4,128)(4,1)S(1)} %copy.25, s32[512,4]{1,0:T(8,128)S(1)} %copy.21), kind=kOutput, calls=%fused_computation.1 | convolution fusion | flops 21102592 | bytes 8527872 | tf_op jit(solution)/shard_map/nsc,nsj->ncj/dot_general | solution.py:19
  52.5 12.8 %copy.26 = f32[512,64,64]{0,2,1:T(8,128)} copy(f32[512,64,64]{2,1,0:T(8,128)} %convert_convert_fusion) | data formatting | bytes 16777216 | tf_op jit(solution)/shard_map/convert_element_type | solution.py:29
  65.3 0.0 copy-start.2
  65.3 0.0 copy-start.3
  65.3 9.0 %copy.27 = f32[512,4096]{1,0:T(8,128)} copy(f32[512,4096]{0,1:T(8,128)} %bitcast.13) | data formatting | bytes 16777216 | tf_op jit(solution)/shard_map/convert_element_type | solution.py:29
  74.3 0.0 copy-done.2
  74.3 0.0 copy-done.3
  74.3 0.6 dynamic-slice
  75.5 0.2 dynamic-update-slice
  75.8 205.7 %all-reduce = bf16[4096]{0:T(1024)(128)(2,1)S(1)} all-reduce(bf16[4096]{0:T(1024)(128)(2,1)S(1)} %dynamic-update-slice), channel_id=1, replica_groups=mesh['enc'=4,'lab'=64] {'lab'}, use_global_device_ids=true, to_apply=%add | all-reduce | flops 4096 | bytes 16384
  281.5 0.0 all-gather.3.cloned.1.call-done
  281.5 0.0 copy-done
  281.5 11.0 %multiply_convert_fusion = bf16[512,4096]{1,0:T(8,128)(2,1)} fusion(f32[512,4096]{1,0:T(8,128)} %copy.27, f32[512,4096]{1,0:T(8,128)} %copy.24, bf16[512,768]{1,0:T(8,128)(2,1)S(1)} %copy-done, bf16[4096,768]{1,0:T(8,128)(2,1)} %all-gather.3.cloned.1.call-done, f32[4096]{0:T(1024)S(1)} %convert_element_type.49), kind=kOutput, calls=%fused_computation | convolution fusion | flops 3235905536 | bytes 28065792 | tf_op jit(solution)/shard_map/dot_general | solution.py:30
  292.5 10.2 %fusion.2 = f32[4096,768]{1,0:T(8,128)} fusion(bf16[512,4096]{1,0:T(8,128)(2,1)} %multiply_convert_fusion, bf16[512,768]{1,0:T(8,128)(2,1)S(1)} %copy-done), kind=kOutput, calls=%fused_computation.11 | convolution fusion | flops 3221225472 | bytes 17563648 | tf_op jit(solution)/shard_map/dot_general | solution.py:64
  302.8 0.0 reduce-scatter.2.cloned.1.call-update
  302.8 8.6 %fusion.3 = f32[512,768]{1,0:T(8,128)} fusion(bf16[512,4096]{1,0:T(8,128)(2,1)} %multiply_convert_fusion, bf16[4096,768]{1,0:T(8,128)(2,1)} %all-gather.3.cloned.1.call-done), kind=kOutput, calls=%fused_computation.12 | convolution fusion | flops 3221225472 | bytes 12058624 | tf_op jit(solution)/shard_map/dot_general | solution.py:34
  311.4 220.2 %reduce-scatter.2.cloned.1.call-done = f32[64,768]{1,0:T(8,128)} async-done(((f32[4096,768]{1,0:T(8,128)}), f32[64,768]{1,0:T(8,128)}) %reduce-scatter.2.cloned.1.call-update) | async-done | bytes 196624 | tf_op jit(solution)/shard_map/reduce_scatter | solution.py:63
  531.6 17.8 %all-gather = f32[256,768]{1,0:T(8,128)S(1)} all-gather(f32[64,768]{1,0:T(8,128)} %reduce-scatter.2.cloned.1.call-done), channel_id=2, replica_groups=mesh['enc'=4,'lab'=64] {'enc'}, dimensions={0}, use_global_device_ids=true | all-gather | bytes 983040 | tf_op jit(solution)/shard_map/all_gather | solution.py:72
  549.5 0.7 broadcast_multiply_fusion
  (4 shorter events, 0.1 us)
Async XLA Ops:
  7.2 274.4 %copy-start = (bf16[512,768]{1,0:T(8,128)(2,1)S(1)}, bf16[512,768]{1,0:T(8,128)(2,1)}, u32[]{:S(2)}) copy-start(bf16[512,768]{1,0:T(8,128)(2,1)} %param.7) | copy-start | bytes 2359300
  7.2 274.3 %all-gather.3.cloned.1.call-start = ((), (), s32[]{:S(2)}) async-start(), calls=%async_computation.1 | async-start | bytes 6389760 | tf_op jit(solution)/shard_map/all_gather | solution.py:58
  8.9 522.7 %reduce-scatter.2.cloned.1.call-start = ((), (), s32[]{:S(2)}) async-start(), calls=%async_computation.2 | async-start | bytes 12779520 | tf_op jit(solution)/shard_map/reduce_scatter | solution.py:63
  34.4 8.9 %copy-start.1 = (s32[512,4]{0,1:T(4,128)S(1)}, s32[512,4]{0,1:T(4,128)}, u32[]{:S(2)}) copy-start(s32[512,4]{0,1:T(4,128)} %param.12) | copy-start | bytes 24580
  65.3 9.0 %copy-start.2 = (s32[64]{0:T(128)S(1)}, s32[64]{0:T(128)}, u32[]{:S(2)}) copy-start(s32[64]{0:T(128)} %param.9) | copy-start | bytes 772
  65.3 9.0 %copy-start.3 = (u32[256]{0:T(256)S(1)}, u32[256]{0:T(256)}, u32[]{:S(2)}) copy-start(u32[256]{0:T(256)} %constant.8) | copy-start | bytes 3076
Sparse Core Ops, SparseCore 0:
  12.3 104.1 all-gather.2
  302.9 228.6 reduce-scatter.1
